TPU v7x, 32 devices: a whole 2x2x4 slice. The times are simulated.
32 devices in a mesh: groups: 2 (over x), ctx: 16 (over z, y, core).
Axes of the slice: x: 2, y: 2, z: 4, core: 2. Of those that a mesh axis runs over, the one named last changes fastest.
Arguments:
- queries: bfloat16 [4096, 1024], P(('groups', 'ctx')), parts along dimension 0, may hold values from -100 to 100
- encoder_rows: bfloat16 [3072, 2048], P(('groups', 'ctx')), parts along dimension 0, may hold values from -6 to 6
- key_weight: bfloat16 [2048, 1024], replicated, may hold values from -0.125 to 0.125
- value_weight: bfloat16 [2048, 1024], replicated, may hold values from -0.125 to 0.125
- out_weight: bfloat16 [1024, 2048], P(None, 'ctx'), may hold values from -0.1875 to 0.1875
Outputs:
- attended: bfloat16 [4096, 2048], P(('groups', 'ctx')), parts along dimension 0
There are 2 independent parts, one for each index of `groups`. A program takes and returns all parts, laid end to end along the dimension named above; an argument that names none is the same for every part. Nothing has to cross between parts.
All inputs are finite; a program needn't handle non-finite values.
Results may differ from a plain program's by a relative error of at most 0.009.
The roundings to bfloat16 on the way count: a program that leaves them out, or rounds other values in their place, can miss the bound.
Values may be sent and summed in bfloat16 or wider, within the bound.
A program may use at most 192 MiB of HBM per device.

v0:
```python
import functools
import math

import jax
import jax.numpy as jnp
from jax import lax
from jax.experimental import pallas as pl
from jax.experimental.pallas import tpu as pltpu
from jax.sharding import PartitionSpec as P

HEADS = 16
DH = 64
PAIR = 2 * DH
MESH = pl.DeviceIdType.MESH
LOG2E = 1.4426950408889634


def kernel(
    groups, n, plane, chunks,
    q_ref, e_ref, kw_hbm, vw_hbm, ow_ref, o_ref,
    kw, vw, qpack, kvpack, qall, kvall, cpack, call, ctx, wall,
    load_sem, own_sem, q_send, q_recv, kv_send, kv_recv, c_send, c_recv,
    z_send, z_recv, y_send, y_recv, x_send, x_recv, b_send, b_recv,
):
    grp = lax.axis_index("groups")
    me = lax.axis_index("ctx")
    rows = q_ref.shape[0]
    enc = e_ref.shape[0]
    depth = ow_ref.shape[0]
    copies = n // HEADS
    share = rows // copies
    half = share // 2
    part = depth // groups
    layers = n // plane
    zed = me // plane
    spot = me % plane
    far = plane // 2
    over = zed * plane + (spot + far) % plane
    mate = zed * plane + (spot // 2) * 2 + (1 - spot % 2)

    def loads(j):
        width = kw.shape[2]
        cols = pl.ds(j * width, width)
        return (
            pltpu.make_async_copy(kw_hbm.at[:, cols], kw.at[j], load_sem.at[j]),
            pltpu.make_async_copy(vw_hbm.at[:, cols], vw.at[j], load_sem.at[chunks + j]),
        )

    for j in range(chunks):
        for copy in loads(j):
            copy.start()
    own = pltpu.make_async_copy(ow_ref, wall.at[me], own_sem)
    own.start()

    barrier = pltpu.get_barrier_semaphore()

    def greet(i, carry):
        pl.semaphore_signal(
            barrier, inc=1, device_id=(grp, (me + i) % n), device_id_type=MESH
        )
        return carry

    lax.fori_loop(1, n, greet, 0)
    for g in range(1, groups):
        pl.semaphore_signal(
            barrier, inc=1, device_id=((grp + g) % groups, me), device_id_type=MESH
        )

    for d in range(n):
        r0, c0 = (d // HEADS) * share, (d % HEADS) * DH
        qpack[d] = jnp.concatenate(
            [q_ref[r0 : r0 + half, c0 : c0 + DH], q_ref[r0 + half : r0 + share, c0 : c0 + DH]],
            axis=1,
        )
    def remote(src, dst, send, recv, to):
        return pltpu.make_async_remote_copy(
            src_ref=src, dst_ref=dst, send_sem=send, recv_sem=recv,
            device_id=to, device_id_type=MESH,
        )

    def q_copy(d, s):
        return remote(qpack.at[d], qall.at[s], q_send.at[d], q_recv.at[s], (grp, d))

    def kv_copy(d, s):
        return remote(
            kvpack.at[d % HEADS], kvall.at[pl.ds(s * enc, enc)],
            kv_send.at[d], kv_recv.at[s], (grp, d),
        )

    def c_copy(d, s):
        return remote(cpack.at[d], call.at[s], c_send.at[d], c_recv.at[s], (grp, d))

    mine = pl.ds(grp * part, part)

    def z_copy(src, way):
        block = wall.at[src * plane + spot, mine]
        to = zed + 1 - 2 * way
        return remote(
            block, block, z_send.at[way * layers + src], z_recv.at[src],
            (grp, to * plane + spot),
        )

    def hop(src, way, act):
        @pl.when((zed > 0) if way else (zed + 1 < layers))
        def _():
            act(z_copy(src, way))

    def y_copy(layer, at, to):
        block = wall.at[layer * plane + at, mine]
        return remote(block, block, y_send.at[layer], y_recv.at[layer], (grp, to))

    def near_copy(at, to):
        block = wall.at[zed * plane + at]
        return remote(block, block, y_send.at[zed], y_recv.at[zed], (grp, to))

    def x_copy(layer, side, g, whose):
        at = layer * plane + (spot + side * far) % plane
        block = wall.at[at, pl.ds(whose * part, part)]
        slot = (g * 2 + side) * layers + layer
        return remote(
            block, block, x_send.at[slot], x_recv.at[slot], ((grp + g) % groups, me)
        )

    def b_copy(layer, side, at):
        block = wall.at[layer * plane + (at + side * far) % plane]
        slot = side * layers + layer
        return remote(block, block, b_send.at[slot], b_recv.at[slot], (grp, mate))

    def some(first, last, body):
        def step(i, carry):
            body((me + i) % n)
            return carry

        lax.fori_loop(first, last, step, 0)

    def others(body):
        some(1, n, body)

    def beyond(body):
        def step(i, carry):
            body((zed + i) % layers)
            return carry

        lax.fori_loop(1, layers, step, 0)

    heads = HEADS // chunks
    for j in range(chunks):
        one, two = loads(j)
        one.wait()
        two.wait()
        keys = jnp.dot(e_ref[...], kw[j], preferred_element_type=jnp.float32).astype(jnp.bfloat16)
        values = jnp.dot(e_ref[...], vw[j], preferred_element_type=jnp.float32).astype(jnp.bfloat16)
        for h in range(heads):
            cols = slice(h * DH, (h + 1) * DH)
            kvpack[j * heads + h] = jnp.concatenate([keys[:, cols], values[:, cols]], axis=1)

    own.wait()
    pl.semaphore_wait(barrier, n - 1 + groups - 1)
    hop(zed, 0, lambda copy: copy.start())
    hop(zed, 1, lambda copy: copy.start())
    kvall[pl.ds(me * enc, enc)] = kvpack[me % HEADS]
    qall[me] = qpack[me]

    def sources(k, body):
        for way in range(2):
            src = zed + k if way else zed - k

            @pl.when((src < layers) if way else (src >= 0))
            def _():
                body(src, way)

    def pass_on(src, way):
        z_copy(src, way).wait_recv()
        hop(src, way, lambda copy: copy.start())
        y_copy(src, spot, over).start()

    def pass_x(z, way):
        y_copy(z, (spot + far) % plane, over).wait_recv()
        for g in range(1, groups):
            x_copy(z, 0, g, grp).start()
            x_copy(z, 1, g, grp).start()

    near_copy(spot, over).start()
    steps = layers - 1
    for k in range(1, layers):
        some(n - (n - 1) * (steps - k + 1) * (steps - k + 1) // (steps * steps), n - (n - 1) * (steps - k) * (steps - k) // (steps * steps), lambda d: kv_copy(d, me).start())
        sources(k, pass_on)
        if k > 1:
            sources(k - 1, pass_x)
    others(lambda d: q_copy(d, me).start())
    sources(steps, pass_x)
    near_copy((spot + far) % plane, over).wait_recv()
    others(lambda s: kv_copy(s, s).wait_recv())

    together = 2

    def attend(i, carry):
        whose = [(me + 1 + i * together + j) % n for j in range(together)]
        pieces = []
        for s in whose:

            @pl.when(s != me)
            def _(s=s):
                q_copy(s, s).wait_recv()

            packed = qall[s]
            pieces += [packed[:, :DH], packed[:, DH:]]
        query = jnp.concatenate(pieces, axis=0)
        memory = kvall[...]
        scores = lax.dot_general(
            query, memory[:, :DH], (((1,), (1,)), ((), ())), preferred_element_type=jnp.float32
        )
        top = jnp.max(scores, axis=1, keepdims=True)
        expo = jnp.exp2((scores - top) * (0.125 * LOG2E))
        total = jnp.sum(expo, axis=1, keepdims=True)
        summed = jnp.dot(expo.astype(jnp.bfloat16), memory, preferred_element_type=jnp.float32)
        out = (summed[:, DH:] / total).astype(jnp.bfloat16)
        for j, s in enumerate(whose):
            low = 2 * j * half
            cpack[s] = jnp.concatenate([out[low : low + half], out[low + half : low + share]], axis=1)

            @pl.when(s != me)
            def _(s=s):
                c_copy(s, me).start()

        return carry

    def pass_b(layer):
        b_copy(layer, 0, spot).start()
        b_copy(layer, 1, spot).start()

    def take_x(z):
        for g in range(1, groups):
            x_copy(z, 0, g, (grp + groups - g) % groups).wait_recv()
            x_copy(z, 1, g, (grp + groups - g) % groups).wait_recv()
        pass_b(z)

    pass_b(zed)

    lax.fori_loop(0, n // together, attend, 0)
    beyond(take_x)
    call[me] = cpack[me]
    others(lambda s: c_copy(s, s).wait_recv())
    for c in range(copies):
        for j in range(HEADS // 2):
            one, two = call[c * HEADS + 2 * j], call[c * HEADS + 2 * j + 1]
            r0, cols = c * share, slice(j * PAIR, (j + 1) * PAIR)
            ctx[r0 : r0 + half, cols] = jnp.concatenate([one[:, :DH], two[:, :DH]], axis=1)
            ctx[r0 + half : r0 + share, cols] = jnp.concatenate([one[:, DH:], two[:, DH:]], axis=1)

    def take_b(z):
        mates = mate % plane
        b_copy(z, 0, mates).wait_recv()
        b_copy(z, 1, mates).wait_recv()

    take_b(zed)
    beyond(take_b)
    width = ow_ref.shape[1]
    for d in range(0, n, 2):
        pair = jnp.concatenate([wall[d], wall[d + 1]], axis=1)
        o_ref[:, d * width : (d + 2) * width] = jnp.dot(
            ctx[...], pair, preferred_element_type=jnp.float32
        ).astype(jnp.bfloat16)

    def sent(d):
        q_copy(d, me).wait_send()
        kv_copy(d, me).wait_send()
        c_copy(d, me).wait_send()

    others(sent)

    def sent_layer(z):
        y_copy(z, spot, over).wait_send()
        for g in range(1, groups):
            x_copy(z, 0, g, grp).wait_send()
            x_copy(z, 1, g, grp).wait_send()
        b_copy(z, 0, spot).wait_send()
        b_copy(z, 1, spot).wait_send()

    beyond(sent_layer)

    def sent_hop(z, carry):
        @pl.when(z <= zed)
        def _():
            hop(z, 0, lambda copy: copy.wait_send())

        @pl.when(z >= zed)
        def _():
            hop(z, 1, lambda copy: copy.wait_send())

        return carry

    lax.fori_loop(0, layers, sent_hop, 0)
    near_copy(spot, over).wait_send()
    b_copy(zed, 0, spot).wait_send()
    b_copy(zed, 1, spot).wait_send()


def per_device(groups, n, queries, encoder_rows, key_weight, value_weight, out_weight):
    rows = queries.shape[0]
    enc, model = encoder_rows.shape
    wide = key_weight.shape[1]
    depth, width = out_weight.shape
    plane = math.gcd(n, 4)
    layers = n // plane
    chunks = 4
    half = rows // (n // HEADS) // 2
    bf16 = jnp.bfloat16
    dma = lambda k: pltpu.SemaphoreType.DMA((k,))
    vmem = pl.BlockSpec(memory_space=pltpu.VMEM)
    hbm = pl.BlockSpec(memory_space=pl.ANY)
    return pl.pallas_call(
        functools.partial(kernel, groups, n, plane, chunks),
        out_shape=jax.ShapeDtypeStruct((rows, n * width), bf16),
        in_specs=[vmem, vmem, hbm, hbm, vmem],
        out_specs=vmem,
        scratch_shapes=[
            pltpu.VMEM((chunks, model, wide // chunks), bf16),
            pltpu.VMEM((chunks, model, wide // chunks), bf16),
            pltpu.VMEM((n, half, PAIR), bf16),
            pltpu.VMEM((HEADS, enc, PAIR), bf16),
            pltpu.VMEM((n, half, PAIR), bf16),
            pltpu.VMEM((n * enc, PAIR), bf16),
            pltpu.VMEM((n, half, PAIR), bf16),
            pltpu.VMEM((n, half, PAIR), bf16),
            pltpu.VMEM((rows, depth), bf16),
            pltpu.VMEM((n, depth, width), bf16),
            dma(2 * chunks),
            pltpu.SemaphoreType.DMA,
            dma(n), dma(n), dma(n), dma(n), dma(n), dma(n),
            dma(2 * layers), dma(layers), dma(layers), dma(layers),
            dma(2 * groups * layers), dma(2 * groups * layers),
            dma(2 * layers), dma(2 * layers),
        ],
        compiler_params=pltpu.CompilerParams(
            collective_id=0, has_side_effects=True, vmem_limit_bytes=60 * 1024 * 1024
        ),
    )(queries, encoder_rows, key_weight, value_weight, out_weight)


def solution(mesh):
    groups, n = mesh.shape["groups"], mesh.shape["ctx"]
    return jax.shard_map(
        functools.partial(per_device, groups, n),
        mesh=mesh,
        in_specs=(P(("groups", "ctx"), None), P(("groups", "ctx"), None), P(), P(), P(None, "ctx")),
        out_specs=P(("groups", "ctx"), None),
        check_vma=False,
    )
```

profile of v0, /device:TPU:0, one launch (start us, length us, event | category | flops | bytes accessed | tf_op | source)
XLA Modules:
  0.0 48.8 jit_solution(16912918297598895151)
XLA Ops:
  0.0 46.9 %shard_map.55 = bf16[128,2048]{1,0:T(8,128)(2,1)} custom-call(bf16[128,1024]{1,0:T(8,128)(2,1)} %q_ref.1, bf16[96,2048]{1,0:T(8,128)(2,1)} %e_ref.1, bf16[2048,1024]{1,0:T(8,128)(2,1)} %kw_hbm.1, bf16[2048,1024]{1,0:T(8,128)(2,1)} %vw_hbm.1, bf16[1024,128]{1,0:T(8,128)(2,1)} %ow_ref.1), custom_call_target="tpu_custom_call" | custom-call | tf_op jit(solution)/shard_map/pallas_call | solution.py:312
  46.9 1.9 %copy.7 = bf16[128,2048]{1,0:T(8,128)(2,1)} copy(bf16[128,2048]{1,0:T(8,128)(2,1)} %shard_map.55) | data formatting | bytes 1048576
where the time goes:
time: 48.9 us; the launch traced here: 48.8 us
  Pallas kernels  46.9 us (96%)
  local copies, waits for them, and re-layouts  1.88 us (4%)
    pallas_call x1, Pallas kernels, per_device(): pl.pallas_call(functools.partial(kernel, groups, n, plane, chunks), out_s...  46.9 us
    unnamed x1, local copies, waits for them, and re-layouts  1.88 us

commit v1 on v0

--- a/solution.py
+++ b/solution.py
@@ -13,13 +13,14 @@
 PAIR = 2 * DH
 MESH = pl.DeviceIdType.MESH
 LOG2E = 1.4426950408889634
+SPLIT = 2
 
 
 def kernel(
     groups, n, plane, chunks,
-    q_ref, e_ref, kw_hbm, vw_hbm, ow_ref, o_ref,
-    kw, vw, qpack, kvpack, qall, kvall, cpack, call, ctx, wall,
-    load_sem, own_sem, q_send, q_recv, kv_send, kv_recv, c_send, c_recv,
+    q_hbm, e_hbm, kw_hbm, vw_hbm, ow_ref, o_ref,
+    q_ref, e_ref, kw, vw, qpack, kvpack, qall, kvall, cpack, call, ctx, wall,
+    load_sem, own_sem, in_sem, q_send, q_recv, kv_send, kv_recv, c_send, c_recv,
     z_send, z_recv, y_send, y_recv, x_send, x_recv, b_send, b_recv,
 ):
     grp = lax.axis_index("groups")
@@ -46,12 +47,6 @@
             pltpu.make_async_copy(vw_hbm.at[:, cols], vw.at[j], load_sem.at[chunks + j]),
         )
 
-    for j in range(chunks):
-        for copy in loads(j):
-            copy.start()
-    own = pltpu.make_async_copy(ow_ref, wall.at[me], own_sem)
-    own.start()
-
     barrier = pltpu.get_barrier_semaphore()
 
     def greet(i, carry):
@@ -66,6 +61,19 @@
             barrier, inc=1, device_id=((grp + g) % groups, me), device_id_type=MESH
         )
 
+    take_q = pltpu.make_async_copy(q_hbm, q_ref, in_sem.at[0])
+    take_e = pltpu.make_async_copy(e_hbm, e_ref, in_sem.at[1])
+    own = pltpu.make_async_copy(ow_ref, wall.at[me], own_sem)
+    take_q.start()
+    take_e.start()
+    for copy in loads(0):
+        copy.start()
+    own.start()
+    for j in range(1, chunks):
+        for copy in loads(j):
+            copy.start()
+
+    take_q.wait()
     for d in range(n):
         r0, c0 = (d // HEADS) * share, (d % HEADS) * DH
         qpack[d] = jnp.concatenate(
@@ -90,33 +98,39 @@
     def c_copy(d, s):
         return remote(cpack.at[d], call.at[s], c_send.at[d], c_recv.at[s], (grp, d))
 
-    mine = pl.ds(grp * part, part)
-
-    def z_copy(src, way):
-        block = wall.at[src * plane + spot, mine]
+    split = SPLIT
+    piece = part // split
+
+    def rows_of(whose, p):
+        return pl.ds(whose * part + p * piece, piece)
+
+    def z_copy(src, way, p):
+        block = wall.at[src * plane + spot, rows_of(grp, p)]
         to = zed + 1 - 2 * way
         return remote(
-            block, block, z_send.at[way * layers + src], z_recv.at[src],
+            block, block, z_send.at[(way * layers + src) * split + p], z_recv.at[src * split + p],
             (grp, to * plane + spot),
         )
 
-    def hop(src, way, act):
+    def hop(src, way, p, act):
         @pl.when((zed > 0) if way else (zed + 1 < layers))
         def _():
-            act(z_copy(src, way))
-
-    def y_copy(layer, at, to):
-        block = wall.at[layer * plane + at, mine]
-        return remote(block, block, y_send.at[layer], y_recv.at[layer], (grp, to))
+            act(z_copy(src, way, p))
+
+    def y_copy(layer, at, to, p):
+        block = wall.at[layer * plane + at, rows_of(grp, p)]
+        slot = layer * split + p
+        return remote(block, block, y_send.at[slot], y_recv.at[slot], (grp, to))
 
     def near_copy(at, to):
         block = wall.at[zed * plane + at]
-        return remote(block, block, y_send.at[zed], y_recv.at[zed], (grp, to))
-
-    def x_copy(layer, side, g, whose):
+        slot = zed * split
+        return remote(block, block, y_send.at[slot], y_recv.at[slot], (grp, to))
+
+    def x_copy(layer, side, g, whose, p):
         at = layer * plane + (spot + side * far) % plane
-        block = wall.at[at, pl.ds(whose * part, part)]
-        slot = (g * 2 + side) * layers + layer
+        block = wall.at[at, rows_of(whose, p)]
+        slot = ((g * 2 + side) * layers + layer) * split + p
         return remote(
             block, block, x_send.at[slot], x_recv.at[slot], ((grp + g) % groups, me)
         )
@@ -143,6 +157,17 @@
 
         lax.fori_loop(1, layers, step, 0)
 
+    def begin():
+        own.wait()
+        pl.semaphore_wait(barrier, n - 1 + groups - 1)
+        for p in range(split):
+            hop(zed, 0, p, lambda copy: copy.start())
+            hop(zed, 1, p, lambda copy: copy.start())
+        near_copy(spot, over).start()
+        b_copy(zed, 0, spot).start()
+
+    begin()
+    take_e.wait()
     heads = HEADS // chunks
     for j in range(chunks):
         one, two = loads(j)
@@ -154,13 +179,6 @@
             cols = slice(h * DH, (h + 1) * DH)
             kvpack[j * heads + h] = jnp.concatenate([keys[:, cols], values[:, cols]], axis=1)
 
-    own.wait()
-    pl.semaphore_wait(barrier, n - 1 + groups - 1)
-    hop(zed, 0, lambda copy: copy.start())
-    hop(zed, 1, lambda copy: copy.start())
-    kvall[pl.ds(me * enc, enc)] = kvpack[me % HEADS]
-    qall[me] = qpack[me]
-
     def sources(k, body):
         for way in range(2):
             src = zed + k if way else zed - k
@@ -169,27 +187,53 @@
             def _():
                 body(src, way)
 
+    def send_x(z, side, p):
+        for g in range(1, groups):
+            x_copy(z, side, g, grp, p).start()
+
+    def take_x(z, side):
+        for g in range(1, groups):
+            for p in range(split):
+                x_copy(z, side, g, (grp + groups - g) % groups, p).wait_recv()
+        b_copy(z, side, spot).start()
+
     def pass_on(src, way):
-        z_copy(src, way).wait_recv()
-        hop(src, way, lambda copy: copy.start())
-        y_copy(src, spot, over).start()
+        for p in range(split):
+            z_copy(src, way, p).wait_recv()
+            hop(src, way, p, lambda copy: copy.start())
+            y_copy(src, spot, over, p).start()
+            send_x(src, 0, p)
 
     def pass_x(z, way):
-        y_copy(z, (spot + far) % plane, over).wait_recv()
-        for g in range(1, groups):
-            x_copy(z, 0, g, grp).start()
-            x_copy(z, 1, g, grp).start()
-
-    near_copy(spot, over).start()
+        for p in range(split):
+            y_copy(z, (spot + far) % plane, over, p).wait_recv()
+            send_x(z, 1, p)
+
+    def pass_b(z, way):
+        take_x(z, 0)
+        take_x(z, 1)
+
+    def pass_near():
+        near_copy((spot + far) % plane, over).wait_recv()
+        b_copy(zed, 1, spot).start()
+
     steps = layers - 1
-    for k in range(1, layers):
-        some(n - (n - 1) * (steps - k + 1) * (steps - k + 1) // (steps * steps), n - (n - 1) * (steps - k) * (steps - k) // (steps * steps), lambda d: kv_copy(d, me).start())
+    def bound(k):
+        return n - (n - 1) * (steps - k) * (steps - k) // (steps * steps)
+
+    for k in range(1, steps):
+        some(bound(k - 1), bound(k), lambda d: kv_copy(d, me).start())
         sources(k, pass_on)
-        if k > 1:
+        if k == 1:
+            pass_near()
+        else:
             sources(k - 1, pass_x)
+    some(bound(steps - 1), n, lambda d: kv_copy(d, me).start())
     others(lambda d: q_copy(d, me).start())
-    sources(steps, pass_x)
-    near_copy((spot + far) % plane, over).wait_recv()
+    sources(steps - 1, pass_x)
+    sources(steps, pass_on)
+    kvall[pl.ds(me * enc, enc)] = kvpack[me % HEADS]
+    qall[me] = qpack[me]
     others(lambda s: kv_copy(s, s).wait_recv())
 
     together = 2
@@ -223,22 +267,15 @@
             def _(s=s):
                 c_copy(s, me).start()
 
+        @pl.when(i == 1)
+        def _():
+            sources(steps, pass_x)
+
         return carry
 
-    def pass_b(layer):
-        b_copy(layer, 0, spot).start()
-        b_copy(layer, 1, spot).start()
-
-    def take_x(z):
-        for g in range(1, groups):
-            x_copy(z, 0, g, (grp + groups - g) % groups).wait_recv()
-            x_copy(z, 1, g, (grp + groups - g) % groups).wait_recv()
-        pass_b(z)
-
-    pass_b(zed)
-
     lax.fori_loop(0, n // together, attend, 0)
-    beyond(take_x)
+    for k in range(1, layers):
+        sources(k, pass_b)
     call[me] = cpack[me]
     others(lambda s: c_copy(s, s).wait_recv())
     for c in range(copies):
@@ -270,10 +307,11 @@
     others(sent)
 
     def sent_layer(z):
-        y_copy(z, spot, over).wait_send()
-        for g in range(1, groups):
-            x_copy(z, 0, g, grp).wait_send()
-            x_copy(z, 1, g, grp).wait_send()
+        for p in range(split):
+            y_copy(z, spot, over, p).wait_send()
+            for g in range(1, groups):
+                x_copy(z, 0, g, grp, p).wait_send()
+                x_copy(z, 1, g, grp, p).wait_send()
         b_copy(z, 0, spot).wait_send()
         b_copy(z, 1, spot).wait_send()
 
@@ -282,11 +320,13 @@
     def sent_hop(z, carry):
         @pl.when(z <= zed)
         def _():
-            hop(z, 0, lambda copy: copy.wait_send())
+            for p in range(split):
+                hop(z, 0, p, lambda copy: copy.wait_send())
 
         @pl.when(z >= zed)
         def _():
-            hop(z, 1, lambda copy: copy.wait_send())
+            for p in range(split):
+                hop(z, 1, p, lambda copy: copy.wait_send())
 
         return carry
 
@@ -304,6 +344,7 @@
     plane = math.gcd(n, 4)
     layers = n // plane
     chunks = 4
+    split = SPLIT
     half = rows // (n // HEADS) // 2
     bf16 = jnp.bfloat16
     dma = lambda k: pltpu.SemaphoreType.DMA((k,))
@@ -312,9 +353,11 @@
     return pl.pallas_call(
         functools.partial(kernel, groups, n, plane, chunks),
         out_shape=jax.ShapeDtypeStruct((rows, n * width), bf16),
-        in_specs=[vmem, vmem, hbm, hbm, vmem],
+        in_specs=[hbm, hbm, hbm, hbm, hbm],
         out_specs=vmem,
         scratch_shapes=[
+            pltpu.VMEM((rows, wide), bf16),
+            pltpu.VMEM((enc, model), bf16),
             pltpu.VMEM((chunks, model, wide // chunks), bf16),
             pltpu.VMEM((chunks, model, wide // chunks), bf16),
             pltpu.VMEM((n, half, PAIR), bf16),
@@ -327,9 +370,10 @@
             pltpu.VMEM((n, depth, width), bf16),
             dma(2 * chunks),
             pltpu.SemaphoreType.DMA,
+            dma(2),
             dma(n), dma(n), dma(n), dma(n), dma(n), dma(n),
-            dma(2 * layers), dma(layers), dma(layers), dma(layers),
-            dma(2 * groups * layers), dma(2 * groups * layers),
+            dma(2 * layers * split), dma(layers * split), dma(layers * split), dma(layers * split),
+            dma(2 * groups * layers * split), dma(2 * groups * layers * split),
             dma(2 * layers), dma(2 * layers),
         ],
         compiler_params=pltpu.CompilerParams(

time: 48.9 us -> 44.2 us (0.904)
  Pallas kernels: 46.9 us -> 42 us
    pallas_call x1, Pallas kernels: 46.9 us -> 42 us  [per_device(): pl.pallas_call(functools.partial(kernel, groups, n, plane, chunks), out_s...]
where the time goes in v1:
time: 44.2 us; the launch traced here: 43.9 us
  Pallas kernels  42 us (95%)
  local copies, waits for them, and re-layouts  1.88 us (4%)
    pallas_call x1, Pallas kernels, per_device(): pl.pallas_call(functools.partial(kernel, groups, n, plane, chunks), out_s...  42 us
    unnamed x1, local copies, waits for them, and re-layouts  1.88 us

profile of v1, /device:TPU:0, one launch (start us, length us, event | category | flops | bytes accessed | tf_op | source)
XLA Modules:
  0.0 43.9 jit_solution(3959899124913914195)
XLA Ops:
  0.0 42.0 %shard_map.55 = bf16[128,2048]{1,0:T(8,128)(2,1)} custom-call(bf16[128,1024]{1,0:T(8,128)(2,1)} %q_hbm.1, bf16[96,2048]{1,0:T(8,128)(2,1)} %e_hbm.1, bf16[2048,1024]{1,0:T(8,128)(2,1)} %kw_hbm.1, bf16[2048,1024]{1,0:T(8,128)(2,1)} %vw_hbm.1, bf16[1024,128]{1,0:T(8,128)(2,1)} %ow_ref.1), custom_call_target="tpu_custom_call" | custom-call | tf_op jit(solution)/shard_map/pallas_call | solution.py:353
  42.0 1.9 %copy.7 = bf16[128,2048]{1,0:T(8,128)(2,1)} copy(bf16[128,2048]{1,0:T(8,128)(2,1)} %shard_map.55) | data formatting | bytes 1048576
